TPU v7x, 32 devices: a whole 2x2x4 slice. The times are simulated.
32 devices in a mesh: leaf: 8 (over z, x), task: 4 (over y, core).
Axes of the slice: x: 2, y: 2, z: 4, core: 2. Of those that a mesh axis runs over, the one named last changes fastest.
Arguments:
- points: bfloat16 [131072, 64], P(('leaf', 'task')), may hold values from -6 to 6
- weights: bfloat16 [131072, 64], P(('leaf', 'task')), may hold values from -4 to 4
- point_order: int32 [8, 4, 4096], P('leaf', 'task'), may hold values from 0 to 4095, each once within a row
- node_order: int32 [8, 4, 4096], P('leaf', 'task'), may hold values from 0 to 4095, each once within a row
- merge_order: int32 [8, 4, 2, 1024], P('leaf', 'task'), may hold values from 0 to 1023, as said below
- far_list: int32 [8, 4, 4, 3], P('leaf', 'task'), may hold values 0 or 1
- task_target: int32 [8, 4, 4, 1], P('leaf', 'task'), may hold values from -1 to 3, as said below
- task_source: int32 [8, 4, 4, 1], P('leaf', 'task'), may hold values from 0 to 3
Outputs:
- potentials: float32 [131072, 64], P(('leaf', 'task'))
Inputs may be any that keep to these rules, and one draw needn't show every extreme that they name: `merge_order`: each row is a permutation of 0 to 1023; rows [i, j, b] are equal for all i with the same i // 2 ** (b + 1). `task_target`: -1 marks an empty slot; every device of every draw has a slab toward which all 1 slots are used.
All inputs are finite; a program needn't handle non-finite values. No bound on the sum of `far_list` on one device may be relied on, other than what follows from the above.
Results may differ from a plain program's by a relative error of at most 0.002.
Values may be sent and summed in bfloat16 or wider, within the bound.
A program may use at most 64 MiB of HBM per device.

v0:
```python
import functools
import math

import jax
import jax.numpy as jnp
from jax import lax
from jax.experimental import pallas as pl
from jax.experimental.pallas import tpu as pltpu
from jax.sharding import PartitionSpec as P

SKEL = 512
KERNEL_SCALE = 1.5
LANES = 128
BF = jnp.bfloat16
F32 = jnp.float32

VMEM = pl.BlockSpec(memory_space=pltpu.VMEM)
HBM = pl.BlockSpec(memory_space=pltpu.HBM)
MESH = pl.DeviceIdType.MESH
NT = (((1,), (1,)), ((), ()))
GROUP = 64
TILE = 512


def scale_of(features):
    return KERNEL_SCALE / features * math.log2(math.e)


def bias_of(features):
    return float(int(64 / scale_of(features)) // 16 * 16)


def pieces(norm):
    first = norm.astype(BF).astype(F32)
    left = norm - first
    second = left.astype(BF).astype(F32)
    third = left - second
    return first, second, third


def columns_form(points, width, left, bias=0.0):
    features, count = points.shape
    first, second, third = pieces(jnp.sum(points * points, axis=0, keepdims=True))
    lines = lax.broadcasted_iota(jnp.int32, (8, count), 0)
    at = 0 if left else 3
    ones = 3 - at
    tail = jnp.where((lines >= ones) & (lines < ones + 3), 1.0, 0.0)
    tail = jnp.where(lines == at, -first, tail)
    tail = jnp.where(lines == at + 1, -second, tail)
    tail = jnp.where(lines == at + 2, -third, tail)
    tail = jnp.where(lines == 6, bias if left else 1.0, tail)
    rest = jnp.zeros((width - features - 8, count), F32)
    return jnp.concatenate([points + points if left else points, tail, rest], axis=0)


def dense_of(exponent, features):
    return jnp.exp2(exponent * scale_of(features))


def kept_table(index, count):
    lanes = lax.broadcasted_iota(jnp.int32, index.shape, 1)
    high = jnp.where(index // LANES == lanes, 1.0, 0.0).T.astype(BF)
    low = jnp.where(index % LANES == lanes, 1.0, 0.0).astype(BF)
    return 1.0 - jnp.dot(high, low, preferred_element_type=F32)


def kept_row(table, start, count):
    rows = [table[at : at + 1, :] for at in range(start // LANES, (start + count) // LANES)]
    return jnp.concatenate(rows, axis=1)


def pick_rows(index_of, rows_ref, skel_ref, index_ref):
    width = rows_ref.shape[1]

    def pick(step, carry):
        base = pl.multiple_of(step * GROUP, GROUP)
        found = [index_of(base + inner) for inner in range(GROUP)]
        rows = [rows_ref[index][None] for index in found]
        for inner, (index, row) in enumerate(zip(found, rows)):
            skel_ref[pl.ds(base + inner, 1), :] = row
            index_ref[pl.ds(base + inner, 1), :] = jnp.full((1, width), index, jnp.int32)
        return carry

    lax.fori_loop(0, SKEL // GROUP, pick, 0)


def run_tiles(features, tiles):
    held = None
    for exponent, use in tiles:
        value = exponent()
        if held is not None:
            held[1](dense_of(held[0], features).astype(BF))
        held = (value, use)
    held[1](dense_of(held[0], features).astype(BF))


def chain_kernel(features, levels, slabs, points_in, weights_in, order_in, node_order_in, merge_in,
                 far_in, source_in, target_in,
                 out_ref, near_out_ref, left_ref, last_right_ref, last_weight_ref,
                 points_ref, weights_ref, rows_ref, picked_ref, right_ref, skel_ref, index_ref,
                 dense_ref, part_ref, total_ref, tree_ref, pt_ref, pt_held, wt_ref, wt_held,
                 pair_pt, pair_wt, pair_rows, spread_ref, near_right_ref, far_right_ref,
                 asked_ref, send_ref, near_ref,
                 order_ref, node_order_ref, merge_ref, far_ref, target_ref, source_ref,
                 input_sem, pt_send, pt_recv, wt_send, wt_recv, ask_send, ask_recv, near_send, near_recv):
    loads = [
        pltpu.make_async_copy(source, target, input_sem.at[at])
        for at, (source, target) in enumerate([
            (points_in, points_ref),
            (weights_in, weights_ref),
            (order_in, order_ref),
            (node_order_in, node_order_ref),
            (merge_in, merge_ref),
            (far_in, far_ref),
            (source_in, source_ref),
            (target_in, target_ref),
        ])
    ]
    for load in loads:
        load.start()
    region = lax.axis_index("leaf")
    slab = lax.axis_index("task")
    count = rows_ref.shape[0]
    width = rows_ref.shape[1]
    leaves = left_ref.shape[0]
    leaf = count // leaves
    cap = source_ref.shape[0]
    chunks = count // SKEL

    def bit(level):
        return region // 2**level % 2

    def sibling(level):
        return region + (1 - 2 * bit(level)) * 2**level

    def ahead(step):
        return lax.rem(slab + step, slabs)

    def behind(step):
        return lax.rem(slab + slabs - step, slabs)

    barrier = pltpu.get_barrier_semaphore()
    for level in range(levels):
        pl.semaphore_signal(barrier, inc=1, device_id=(sibling(level), slab), device_id_type=MESH)
    for step in range(1, slabs):
        pl.semaphore_signal(barrier, inc=1, device_id=(region, ahead(step)), device_id_type=MESH)

    def to_sibling(level, source, target, send, recv):
        return pltpu.make_async_remote_copy(
            src_ref=source.at[level],
            dst_ref=target.at[level],
            send_sem=send.at[level],
            recv_sem=recv.at[level],
            device_id=(sibling(level), slab),
            device_id_type=MESH,
        )

    def pt_copy(level):
        return to_sibling(level, pt_ref, pt_held, pt_send, pt_recv)

    def wt_copy(level):
        return to_sibling(level, wt_ref, wt_held, wt_send, wt_recv)

    def ask_copy(step):
        return pltpu.make_async_remote_copy(
            src_ref=source_ref,
            dst_ref=asked_ref.at[step],
            send_sem=ask_send.at[step],
            recv_sem=ask_recv.at[step],
            device_id=(region, ahead(step)),
            device_id_type=MESH,
        )

    def near_copy(step):
        return pltpu.make_async_remote_copy(
            src_ref=send_ref.at[step],
            dst_ref=near_ref.at[step],
            send_sem=near_send.at[step],
            recv_sem=near_recv.at[step],
            device_id=(region, behind(step)),
            device_id_type=MESH,
        )

    for load in loads:
        load.wait()
    for at in range(chunks):
        part = points_ref[:, at * SKEL : (at + 1) * SKEL].astype(F32)
        both = jnp.concatenate(
            [part, weights_ref[:, at * SKEL : (at + 1) * SKEL].astype(F32)], axis=0
        )
        rows_ref[at * SKEL : (at + 1) * SKEL, :] = both.T
        right_ref[at] = columns_form(part, width, False).astype(BF)
    pick_rows(lambda at: order_ref[node_order_ref[at]], rows_ref, skel_ref, index_ref)
    skel = skel_ref[...].T
    pt_ref[0] = skel[:features].astype(BF)
    pl.semaphore_wait(barrier, levels + slabs - 1)
    pt_copy(0).start()
    for step in range(1, slabs):
        ask_copy(step).start()

    left = columns_form(skel[:features], width, True, bias_of(features)).T.astype(BF)
    table = kept_table(index_ref[...], count)
    total_ref[...] = skel[features:]

    def gather(at):
        for inner in range(SKEL):
            picked_ref[at * SKEL + inner : at * SKEL + inner + 1, :] = rows_ref[
                order_ref[at * SKEL + inner]
            ][None]

    def absorb(at):
        total_ref[...] += lax.dot_general(
            part_ref[at % 2], dense_ref[at % 2], NT, preferred_element_type=F32
        )

    for at in range(chunks):
        gather(at)
        dense = dense_of(jnp.dot(left, right_ref[at], preferred_element_type=F32), features)
        if at > 0:
            absorb(at - 1)
        share = kept_row(table, at * SKEL, SKEL) / jnp.sum(dense, axis=0, keepdims=True)
        dense_ref[at % 2] = dense.astype(BF)
        part_ref[at % 2] = (
            weights_ref[:, at * SKEL : (at + 1) * SKEL].astype(F32) * share
        ).astype(BF)
    absorb(chunks - 1)
    wt_ref[0] = total_ref[...].astype(BF)
    wt_copy(0).start()

    for one in range(leaves):
        for start in range(0, leaf, SKEL):
            turn = picked_ref[one * leaf + start : one * leaf + start + SKEL, :].T
            tree_ref[one, :, start : start + SKEL] = turn.astype(BF)
            left_ref[one, :, start : start + SKEL] = columns_form(
                turn[:features], width, True
            ).astype(BF)

    def fill(slot_ref, step, table):
        own = lax.broadcasted_iota(jnp.int32, table.shape, 1) == slab
        place = lax.broadcasted_iota(jnp.int32, table.shape, 0)
        for one in range(cap):
            wanted = jnp.max(
                jnp.where(own & (place == one), table, 0).astype(F32), axis=(0, 1), keepdims=True
            )
            for start in range(0, width, 64):
                rows = tree_ref[0, start : start + 64, :].astype(F32)
                for other in range(1, leaves):
                    rows = jnp.where(
                        wanted == other, tree_ref[other, start : start + 64, :].astype(F32), rows
                    )
                slot_ref[step, one, start : start + 64, :] = rows.astype(BF)

    for step in range(1, slabs):
        ask_copy(step).wait_recv()
        fill(send_ref, step, asked_ref[step])
        near_copy(step).start()
    fill(near_ref, 0, source_ref[...])

    def merge_points(level):
        upper = bit(level)
        pair_pt[upper] = pt_ref[level]
        pair_pt[1 - upper] = pt_held[level]
        for half in range(2):
            points = pair_pt[half].astype(F32)
            right_ref[half] = columns_form(points, width, False).astype(BF)
            pair_rows[half * SKEL : (half + 1) * SKEL, :] = columns_form(points, width, True).T
        pick_rows(lambda at: merge_ref[level, at], pair_rows, skel_ref, index_ref)
        pt_ref[level + 1] = (skel_ref[...].T[:features] * 0.5).astype(BF)
        pt_copy(level + 1).start()
        left = skel_ref[...].astype(BF)
        index = index_ref[...]
        table = kept_table(index, 2 * SKEL)
        wide = jnp.concatenate([index] * (SKEL // LANES), axis=1)
        lanes = lax.broadcasted_iota(jnp.int32, wide.shape, 1)
        for half in range(2):
            dense = dense_of(jnp.dot(left, right_ref[half], preferred_element_type=F32), features)
            share = kept_row(table, half * SKEL, SKEL) / jnp.sum(dense, axis=0, keepdims=True)
            spread_ref[half] = jnp.where(wide == lanes + half * SKEL, 1.0, dense * share).astype(BF)

    def merge_weights(level):
        upper = bit(level)
        pair_wt[upper] = wt_ref[level]
        pair_wt[1 - upper] = wt_held[level]
        total = sum(
            lax.dot_general(pair_wt[half], spread_ref[half], NT, preferred_element_type=F32)
            for half in range(2)
        )
        wt_ref[level + 1] = total.astype(BF)
        wt_copy(level + 1).start()

    def near_terms(step):
        for one in range(cap):
            target = jnp.maximum(target_ref[one, ahead(step)], 0)
            for start in range(0, leaf, SKEL):
                points = near_ref[step, one, :features, start : start + SKEL].astype(F32)
                near_right_ref[start : start + SKEL, :] = columns_form(points, width, False).T.astype(BF)

            def tile(begin, start):
                def exponent():
                    return jnp.dot(
                        near_right_ref[start : start + SKEL, :],
                        left_ref[target, :, begin : begin + TILE],
                        preferred_element_type=F32,
                    )

                def use(dense):
                    term = jnp.dot(
                        near_ref[step, one, features:, start : start + SKEL],
                        dense,
                        preferred_element_type=F32,
                    )
                    place = near_out_ref.at[step, one, :, begin : begin + TILE]
                    place[...] = term if start == 0 else place[...] + term

                return exponent, use

            run_tiles(features, [
                tile(begin, start)
                for begin in range(0, leaf, TILE)
                for start in range(0, leaf, SKEL)
            ])

    def far_right(level):
        return columns_form(pt_held[level].astype(F32), width, False).T.astype(BF)

    def far_terms(level):
        far_right_ref[...] = far_right(level)

        def tile(one, begin):
            def exponent():
                return jnp.dot(
                    far_right_ref[...],
                    left_ref[one, :, begin : begin + TILE],
                    preferred_element_type=F32,
                )

            def use(dense):
                weight = (wt_held[level].astype(F32) * far_ref[level, 0, one].astype(F32)).astype(BF)
                term = jnp.dot(weight, dense, preferred_element_type=F32)
                place = out_ref.at[one, :, begin : begin + TILE]
                place[...] = term if level == 0 else place[...] + term

            return exponent, use

        run_tiles(features, [
            tile(one, begin) for one in range(leaves) for begin in range(0, leaf, TILE)
        ])

    def near_ready(step):
        if step > 0:
            near_copy(step).wait_recv()
        near_terms(step)

    steps = iter(range(slabs))
    for level in range(levels - 1):
        pt_copy(level).wait_recv()
        merge_points(level)
        step = next(steps, None)
        if step is not None:
            near_ready(step)
        wt_copy(level).wait_recv()
        merge_weights(level)
    far_terms(0)
    for step in steps:
        near_ready(step)
    for level in range(1, levels - 1):
        far_terms(level)
    pt_copy(levels - 1).wait_recv()
    last_right_ref[...] = far_right(levels - 1)
    wt_copy(levels - 1).wait_recv()
    for one in range(leaves):
        last_weight_ref[one] = (
            wt_held[levels - 1].astype(F32) * far_ref[levels - 1, 0, one].astype(F32)
        ).astype(BF)
    for level in range(levels):
        pt_copy(level).wait_send()
        wt_copy(level).wait_send()
    for step in range(1, slabs):
        ask_copy(step).wait_send()
        near_copy(step).wait_send()


def last_kernel(features, slabs, target_in, right_ref, weight_ref, left_ref, near_ref, prior_ref,
                out_in, sum_ref, target_ref, input_sem, out_sem):
    load = pltpu.make_async_copy(target_in, target_ref, input_sem.at[0])
    load.start()
    leaves, _, leaf = left_ref.shape

    def leave(one):
        return pltpu.make_async_copy(
            sum_ref.at[one], out_in.at[:, pl.ds(one * leaf, leaf)], out_sem.at[one]
        )

    def tile(one, begin):
        def exponent():
            return jnp.dot(
                right_ref[...], left_ref[one, :, begin : begin + TILE], preferred_element_type=F32
            )

        def use(dense):
            place = sum_ref.at[one, :, begin : begin + TILE]
            place[...] += jnp.dot(weight_ref[one], dense, preferred_element_type=F32)

        return exponent, use

    sum_ref[...] = prior_ref[...]
    load.wait()
    for step in range(slabs):
        owner = lax.rem(lax.axis_index("task") + step, slabs)
        for one in range(target_ref.shape[0]):
            target = target_ref[one, owner]

            @pl.when(target >= 0)
            def _():
                sum_ref[target] += near_ref[step, one]

    for one in range(leaves):
        run_tiles(features, [tile(one, begin) for begin in range(0, leaf, TILE)])
        leave(one).start()
    for one in range(leaves):
        leave(one).wait()


def in_hbm(value):
    return pltpu.with_memory_space_constraint(value, pltpu.HBM)


def body(points, weights, point_order, node_order, merge_order, far_list, task_target, task_source):
    count, features = points.shape
    columns = weights.shape[1]
    width = features + columns
    levels = far_list.shape[3]
    leaves = far_list.shape[2]
    leaf = count // leaves
    slabs, cap = task_source.shape[2:]
    far = far_list.transpose(0, 3, 1, 2)[0]
    source = task_source[0, 0].T
    target = task_target[0, 0].T
    inputs = (points.T, weights.T, point_order[0, 0], node_order[0, 0], merge_order[0, 0], far, source, target)
    total, near, left, right, weight = pl.pallas_call(
        functools.partial(chain_kernel, features, levels, slabs),
        out_shape=(
            jax.ShapeDtypeStruct((leaves, columns, leaf), F32),
            jax.ShapeDtypeStruct((slabs, cap, columns, leaf), F32),
            jax.ShapeDtypeStruct((leaves, width, leaf), BF),
            jax.ShapeDtypeStruct((SKEL, width), BF),
            jax.ShapeDtypeStruct((leaves, columns, SKEL), BF),
        ),
        in_specs=[HBM] * 8,
        out_specs=(VMEM,) * 5,
        scratch_shapes=[
            pltpu.VMEM((features, count), BF),
            pltpu.VMEM((columns, count), BF),
            pltpu.VMEM((count, width), F32),
            pltpu.VMEM((count, width), F32),
            pltpu.VMEM((count // SKEL, width, SKEL), BF),
            pltpu.VMEM((SKEL, width), F32),
            pltpu.VMEM((SKEL, width), jnp.int32),
            pltpu.VMEM((2, SKEL, SKEL), BF),
            pltpu.VMEM((2, columns, SKEL), BF),
            pltpu.VMEM((columns, SKEL), F32),
            pltpu.VMEM((leaves, width, leaf), BF),
            pltpu.VMEM((levels, features, SKEL), BF),
            pltpu.VMEM((levels, features, SKEL), BF),
            pltpu.VMEM((levels, columns, SKEL), BF),
            pltpu.VMEM((levels, columns, SKEL), BF),
            pltpu.VMEM((2, features, SKEL), BF),
            pltpu.VMEM((2, columns, SKEL), BF),
            pltpu.VMEM((2 * SKEL, width), F32),
            pltpu.VMEM((2, SKEL, SKEL), BF),
            pltpu.VMEM((leaf, width), BF),
            pltpu.VMEM((SKEL, width), BF),
            pltpu.VMEM((slabs, cap, slabs), jnp.int32),
            pltpu.VMEM((slabs, cap, width, leaf), BF),
            pltpu.VMEM((slabs, cap, width, leaf), BF),
            pltpu.SMEM((count,), jnp.int32),
            pltpu.SMEM((count,), jnp.int32),
            pltpu.SMEM((levels - 1, 2 * SKEL), jnp.int32),
            pltpu.SMEM(far.shape, jnp.int32),
            pltpu.SMEM(target.shape, jnp.int32),
            pltpu.VMEM(source.shape, jnp.int32),
            pltpu.SemaphoreType.DMA((8,)),
            pltpu.SemaphoreType.DMA((levels,)),
            pltpu.SemaphoreType.DMA((levels,)),
            pltpu.SemaphoreType.DMA((levels,)),
            pltpu.SemaphoreType.DMA((levels,)),
            pltpu.SemaphoreType.DMA((slabs,)),
            pltpu.SemaphoreType.DMA((slabs,)),
            pltpu.SemaphoreType.DMA((slabs,)),
            pltpu.SemaphoreType.DMA((slabs,)),
        ],
        compiler_params=pltpu.CompilerParams(
            collective_id=0, has_side_effects=True, vmem_limit_bytes=48 << 20
        ),
        name="chain",
    )(*[in_hbm(one) for one in inputs])
    out = pl.pallas_call(
        functools.partial(last_kernel, features, slabs),
        out_shape=jax.ShapeDtypeStruct((columns, count), F32),
        in_specs=[HBM] + [VMEM] * 5,
        out_specs=HBM,
        scratch_shapes=[
            pltpu.VMEM((leaves, columns, leaf), F32),
            pltpu.SMEM(target.shape, jnp.int32),
            pltpu.SemaphoreType.DMA((1,)),
            pltpu.SemaphoreType.DMA((leaves,)),
        ],
        compiler_params=pltpu.CompilerParams(vmem_limit_bytes=48 << 20),
        name="last",
    )(in_hbm(target), right, weight, left, near, total)
    return out.T


def solution(mesh):
    return jax.shard_map(
        body,
        mesh=mesh,
        in_specs=(
            P(("leaf", "task"), None),
            P(("leaf", "task"), None),
            P("leaf", "task", None),
            P("leaf", "task", None),
            P("leaf", "task", None, None),
            P("leaf", "task", None, None),
            P("leaf", "task", None, None),
            P("leaf", "task", None, None),
        ),
        out_specs=P(("leaf", "task"), None),
        check_vma=False,
    )
```

profile of v0, /device:TPU:0, one launch (start us, length us, event | category | flops | bytes accessed | tf_op | source)
XLA Modules:
  0.0 31.1 jit_solution(16931787699110277192)
XLA Ops:
  0.0 27.4 %chain.1 = (f32[4,64,1024]{2,1,0:T(8,128)S(1)}, f32[4,1,64,1024]{3,2,1,0:T(8,128)S(1)}, bf16[4,128,1024]{2,1,0:T(8,128)(2,1)S(1)}, bf16[512,128]{1,0:T(8,128)(2,1)S(1)}, bf16[4,64,512]{2,1,0:T(8,128)(2,1)S(1)}) custom-call(bf16[64,4096]{1,0:T(8,128)(2,1)} %bitcast.11, bf16[64,4096]{1,0:T(8,128)(2,1)} %bitcast.12, s32[4096]{0:T(1024)} %bitcast.13, ...), custom_call_target="tpu_custom_call" | custom-call | tf_op jit(solution)/shard_map/chain/pallas_call | solution.py:440
  27.5 3.5 %last.1 = f32[64,4096]{1,0:T(8,128)} custom-call(s32[1,4]{1,0:T(1,128)} %bitcast.17, bf16[512,128]{1,0:T(8,128)(2,1)S(1)} %get-tuple-element.10.right_ref, bf16[4,64,512]{2,1,0:T(8,128)(2,1)S(1)} %get-tuple-element.11.weight_ref, bf16[4,128,1024]{2,1,0:T(8,128)(2,1)S(1)} %get-tuple-element.12.left_ref, f32[4,1,64,1024]{3,2,1,0:T(8,128)S(1)} %get-tuple-element.13.near_ref, ...), custom_call_target="tpu_custom_call" | custom-call | tf_op jit(solution)/shard_map/last/pallas_call | solution.py:497
where the time goes:
time: 31.3 us; the launch traced here: 31.1 us
  Pallas kernels  31 us (99%)
    pallas_call x1, Pallas kernels, body(): pl.pallas_call(functools.partial(chain_kernel, features, levels, slabs),...  27.4 us
    pallas_call x1, Pallas kernels, body(): pl.pallas_call(functools.partial(last_kernel, features, slabs), out_shape...  3.51 us

commit v1 on v0

--- a/solution.py
+++ b/solution.py
@@ -18,16 +18,11 @@
 HBM = pl.BlockSpec(memory_space=pltpu.HBM)
 MESH = pl.DeviceIdType.MESH
 NT = (((1,), (1,)), ((), ()))
-GROUP = 64
 TILE = 512
 
 
 def scale_of(features):
     return KERNEL_SCALE / features * math.log2(math.e)
-
-
-def bias_of(features):
-    return float(int(64 / scale_of(features)) // 16 * 16)
 
 
 def pieces(norm):
@@ -38,7 +33,7 @@
     return first, second, third
 
 
-def columns_form(points, width, left, bias=0.0):
+def columns_form(points, width, left):
     features, count = points.shape
     first, second, third = pieces(jnp.sum(points * points, axis=0, keepdims=True))
     lines = lax.broadcasted_iota(jnp.int32, (8, count), 0)
@@ -48,7 +43,6 @@
     tail = jnp.where(lines == at, -first, tail)
     tail = jnp.where(lines == at + 1, -second, tail)
     tail = jnp.where(lines == at + 2, -third, tail)
-    tail = jnp.where(lines == 6, bias if left else 1.0, tail)
     rest = jnp.zeros((width - features - 8, count), F32)
     return jnp.concatenate([points + points if left else points, tail, rest], axis=0)
 
@@ -59,8 +53,8 @@
 
 def kept_table(index, count):
     lanes = lax.broadcasted_iota(jnp.int32, index.shape, 1)
-    high = jnp.where(index // LANES == lanes, 1.0, 0.0).T.astype(BF)
-    low = jnp.where(index % LANES == lanes, 1.0, 0.0).astype(BF)
+    high = jnp.where(lax.shift_right_logical(index, 7) == lanes, 1.0, 0.0).astype(BF).T
+    low = jnp.where((index & (LANES - 1)) == lanes, 1.0, 0.0).astype(BF)
     return 1.0 - jnp.dot(high, low, preferred_element_type=F32)
 
 
@@ -71,17 +65,10 @@
 
 def pick_rows(index_of, rows_ref, skel_ref, index_ref):
     width = rows_ref.shape[1]
-
-    def pick(step, carry):
-        base = pl.multiple_of(step * GROUP, GROUP)
-        found = [index_of(base + inner) for inner in range(GROUP)]
-        rows = [rows_ref[index][None] for index in found]
-        for inner, (index, row) in enumerate(zip(found, rows)):
-            skel_ref[pl.ds(base + inner, 1), :] = row
-            index_ref[pl.ds(base + inner, 1), :] = jnp.full((1, width), index, jnp.int32)
-        return carry
-
-    lax.fori_loop(0, SKEL // GROUP, pick, 0)
+    for at in range(SKEL):
+        index = index_of(at)
+        skel_ref[at : at + 1, :] = rows_ref[index][None]
+        index_ref[at : at + 1, :] = jnp.full((1, width), index, jnp.int32)
 
 
 def run_tiles(features, tiles):
@@ -98,10 +85,10 @@
                  far_in, source_in, target_in,
                  out_ref, near_out_ref, left_ref, last_right_ref, last_weight_ref,
                  points_ref, weights_ref, rows_ref, picked_ref, right_ref, skel_ref, index_ref,
-                 dense_ref, part_ref, total_ref, tree_ref, pt_ref, pt_held, wt_ref, wt_held,
+                 dense_ref, total_ref, tree_ref, pt_ref, pt_held, wt_ref, wt_held,
                  pair_pt, pair_wt, pair_rows, spread_ref, near_right_ref, far_right_ref,
                  asked_ref, send_ref, near_ref,
-                 order_ref, node_order_ref, merge_ref, far_ref, target_ref, source_ref,
+                 order_ref, node_order_ref, merge_ref, far_ref, target_ref, own_ref, source_ref,
                  input_sem, pt_send, pt_recv, wt_send, wt_recv, ask_send, ask_recv, near_send, near_recv):
     loads = [
         pltpu.make_async_copy(source, target, input_sem.at[at])
@@ -114,6 +101,7 @@
             (far_in, far_ref),
             (source_in, source_ref),
             (target_in, target_ref),
+            (source_in, own_ref),
         ])
     ]
     for load in loads:
@@ -184,21 +172,23 @@
     for load in loads:
         load.wait()
     for at in range(chunks):
-        part = points_ref[:, at * SKEL : (at + 1) * SKEL].astype(F32)
         both = jnp.concatenate(
-            [part, weights_ref[:, at * SKEL : (at + 1) * SKEL].astype(F32)], axis=0
-        )
-        rows_ref[at * SKEL : (at + 1) * SKEL, :] = both.T
-        right_ref[at] = columns_form(part, width, False).astype(BF)
+            [
+                points_ref[:, at * SKEL : (at + 1) * SKEL],
+                weights_ref[:, at * SKEL : (at + 1) * SKEL],
+            ],
+            axis=0,
+        )
+        rows_ref[at * SKEL : (at + 1) * SKEL, :] = both.T.astype(F32)
     pick_rows(lambda at: order_ref[node_order_ref[at]], rows_ref, skel_ref, index_ref)
-    skel = skel_ref[...].T
+    skel = skel_ref[...].astype(BF).T.astype(F32)
     pt_ref[0] = skel[:features].astype(BF)
     pl.semaphore_wait(barrier, levels + slabs - 1)
     pt_copy(0).start()
     for step in range(1, slabs):
         ask_copy(step).start()
 
-    left = columns_form(skel[:features], width, True, bias_of(features)).T.astype(BF)
+    left = columns_form(skel[:features], width, True).astype(BF).T
     table = kept_table(index_ref[...], count)
     total_ref[...] = skel[features:]
 
@@ -210,29 +200,30 @@
 
     def absorb(at):
         total_ref[...] += lax.dot_general(
-            part_ref[at % 2], dense_ref[at % 2], NT, preferred_element_type=F32
+            weights_ref[:, at * SKEL : (at + 1) * SKEL],
+            dense_ref[at % 2],
+            NT,
+            preferred_element_type=F32,
         )
 
     for at in range(chunks):
-        gather(at)
-        dense = dense_of(jnp.dot(left, right_ref[at], preferred_element_type=F32), features)
+        right = columns_form(points_ref[:, at * SKEL : (at + 1) * SKEL].astype(F32), width, False)
+        dense = dense_of(jnp.dot(left, right.astype(BF), preferred_element_type=F32), features)
         if at > 0:
             absorb(at - 1)
         share = kept_row(table, at * SKEL, SKEL) / jnp.sum(dense, axis=0, keepdims=True)
-        dense_ref[at % 2] = dense.astype(BF)
-        part_ref[at % 2] = (
-            weights_ref[:, at * SKEL : (at + 1) * SKEL].astype(F32) * share
-        ).astype(BF)
+        dense_ref[at % 2] = (dense * share).astype(BF)
+        gather(at)
     absorb(chunks - 1)
     wt_ref[0] = total_ref[...].astype(BF)
     wt_copy(0).start()
 
     for one in range(leaves):
         for start in range(0, leaf, SKEL):
-            turn = picked_ref[one * leaf + start : one * leaf + start + SKEL, :].T
-            tree_ref[one, :, start : start + SKEL] = turn.astype(BF)
+            turn = picked_ref[one * leaf + start : one * leaf + start + SKEL, :].astype(BF).T
+            tree_ref[one, :, start : start + SKEL] = turn
             left_ref[one, :, start : start + SKEL] = columns_form(
-                turn[:features], width, True
+                turn[:features].astype(F32), width, True
             ).astype(BF)
 
     def fill(slot_ref, step, table):
@@ -242,19 +233,15 @@
             wanted = jnp.max(
                 jnp.where(own & (place == one), table, 0).astype(F32), axis=(0, 1), keepdims=True
             )
-            for start in range(0, width, 64):
-                rows = tree_ref[0, start : start + 64, :].astype(F32)
-                for other in range(1, leaves):
-                    rows = jnp.where(
-                        wanted == other, tree_ref[other, start : start + 64, :].astype(F32), rows
-                    )
-                slot_ref[step, one, start : start + 64, :] = rows.astype(BF)
+            slot_ref[step, one] = sum(
+                tree_ref[other] * jnp.where(wanted == other, 1.0, 0.0).astype(BF)
+                for other in range(leaves)
+            )
 
     for step in range(1, slabs):
         ask_copy(step).wait_recv()
         fill(send_ref, step, asked_ref[step])
         near_copy(step).start()
-    fill(near_ref, 0, source_ref[...])
 
     def merge_points(level):
         upper = bit(level)
@@ -263,9 +250,9 @@
         for half in range(2):
             points = pair_pt[half].astype(F32)
             right_ref[half] = columns_form(points, width, False).astype(BF)
-            pair_rows[half * SKEL : (half + 1) * SKEL, :] = columns_form(points, width, True).T
+            pair_rows[half * SKEL : (half + 1) * SKEL, :] = columns_form(points, width, True).astype(BF).T.astype(F32)
         pick_rows(lambda at: merge_ref[level, at], pair_rows, skel_ref, index_ref)
-        pt_ref[level + 1] = (skel_ref[...].T[:features] * 0.5).astype(BF)
+        pt_ref[level + 1] = (skel_ref[...] * 0.5).astype(BF).T[:features]
         pt_copy(level + 1).start()
         left = skel_ref[...].astype(BF)
         index = index_ref[...]
@@ -291,9 +278,15 @@
     def near_terms(step):
         for one in range(cap):
             target = jnp.maximum(target_ref[one, ahead(step)], 0)
+            if step == 0:
+                origin, place_at = tree_ref, (own_ref[one, slab],)
+            else:
+                origin, place_at = near_ref, (step, one)
             for start in range(0, leaf, SKEL):
-                points = near_ref[step, one, :features, start : start + SKEL].astype(F32)
-                near_right_ref[start : start + SKEL, :] = columns_form(points, width, False).T.astype(BF)
+                points = origin[(*place_at, slice(0, features), slice(start, start + SKEL))]
+                near_right_ref[start : start + SKEL, :] = columns_form(
+                    points.astype(F32), width, False
+                ).astype(BF).T
 
             def tile(begin, start):
                 def exponent():
@@ -304,11 +297,10 @@
                     )
 
                 def use(dense):
-                    term = jnp.dot(
-                        near_ref[step, one, features:, start : start + SKEL],
-                        dense,
-                        preferred_element_type=F32,
-                    )
+                    weight = origin[
+                        (*place_at, slice(features, width), slice(start, start + SKEL))
+                    ]
+                    term = jnp.dot(weight, dense, preferred_element_type=F32)
                     place = near_out_ref.at[step, one, :, begin : begin + TILE]
                     place[...] = term if start == 0 else place[...] + term
 
@@ -321,7 +313,7 @@
             ])
 
     def far_right(level):
-        return columns_form(pt_held[level].astype(F32), width, False).T.astype(BF)
+        return columns_form(pt_held[level].astype(F32), width, False).astype(BF).T
 
     def far_terms(level):
         far_right_ref[...] = far_right(level)
@@ -404,18 +396,19 @@
         return exponent, use
 
     sum_ref[...] = prior_ref[...]
-    load.wait()
-    for step in range(slabs):
-        owner = lax.rem(lax.axis_index("task") + step, slabs)
-        for one in range(target_ref.shape[0]):
-            target = target_ref[one, owner]
-
-            @pl.when(target >= 0)
-            def _():
-                sum_ref[target] += near_ref[step, one]
-
     for one in range(leaves):
         run_tiles(features, [tile(one, begin) for begin in range(0, leaf, TILE)])
+        if one == 0:
+            load.wait()
+            for step in range(slabs):
+                owner = lax.rem(lax.axis_index("task") + step, slabs)
+                for slot in range(target_ref.shape[0]):
+                    target = target_ref[slot, owner]
+
+                    @pl.when(target >= 0)
+                    def _(step=step, slot=slot, target=target):
+                        sum_ref[target] += near_ref[step, slot]
+
         leave(one).start()
     for one in range(leaves):
         leave(one).wait()
@@ -453,11 +446,10 @@
             pltpu.VMEM((columns, count), BF),
             pltpu.VMEM((count, width), F32),
             pltpu.VMEM((count, width), F32),
-            pltpu.VMEM((count // SKEL, width, SKEL), BF),
+            pltpu.VMEM((2, width, SKEL), BF),
             pltpu.VMEM((SKEL, width), F32),
             pltpu.VMEM((SKEL, width), jnp.int32),
             pltpu.VMEM((2, SKEL, SKEL), BF),
-            pltpu.VMEM((2, columns, SKEL), BF),
             pltpu.VMEM((columns, SKEL), F32),
             pltpu.VMEM((leaves, width, leaf), BF),
             pltpu.VMEM((levels, features, SKEL), BF),
@@ -478,8 +470,9 @@
             pltpu.SMEM((levels - 1, 2 * SKEL), jnp.int32),
             pltpu.SMEM(far.shape, jnp.int32),
             pltpu.SMEM(target.shape, jnp.int32),
+            pltpu.SMEM(source.shape, jnp.int32),
             pltpu.VMEM(source.shape, jnp.int32),
-            pltpu.SemaphoreType.DMA((8,)),
+            pltpu.SemaphoreType.DMA((9,)),
             pltpu.SemaphoreType.DMA((levels,)),
             pltpu.SemaphoreType.DMA((levels,)),
             pltpu.SemaphoreType.DMA((levels,)),

time: 31.3 us -> 30.4 us (0.971)
  Pallas kernels: 31 us -> 30.1 us
    pallas_call x1, Pallas kernels: 3.51 us -> 3.05 us  [body(): pl.pallas_call(functools.partial(last_kernel, features, slabs), out_shape...]
    pallas_call x1, Pallas kernels: 27.4 us -> 27.1 us  [body(): pl.pallas_call(functools.partial(chain_kernel, features, levels, slabs),...]
where the time goes in v1:
time: 30.4 us; the launch traced here: 30.3 us
  Pallas kernels  30.1 us (99%)
    pallas_call x1, Pallas kernels, body(): pl.pallas_call(functools.partial(chain_kernel, features, levels, slabs),...  27.1 us
    pallas_call x1, Pallas kernels, body(): pl.pallas_call(functools.partial(last_kernel, features, slabs), out_shape...  3.05 us

profile of v1, /device:TPU:0, one launch (start us, length us, event | category | flops | bytes accessed | tf_op | source)
XLA Modules:
  0.0 30.3 jit_solution(892977321624038674)
XLA Ops:
  0.0 27.1 %chain.1 = (f32[4,64,1024]{2,1,0:T(8,128)S(1)}, f32[4,1,64,1024]{3,2,1,0:T(8,128)S(1)}, bf16[4,128,1024]{2,1,0:T(8,128)(2,1)S(1)}, bf16[512,128]{1,0:T(8,128)(2,1)S(1)}, bf16[4,64,512]{2,1,0:T(8,128)(2,1)S(1)}) custom-call(bf16[64,4096]{1,0:T(8,128)(2,1)} %bitcast.11, bf16[64,4096]{1,0:T(8,128)(2,1)} %bitcast.12, s32[4096]{0:T(1024)} %bitcast.13, ...), custom_call_target="tpu_custom_call" | custom-call | tf_op jit(solution)/shard_map/chain/pallas_call | solution.py:433
  27.1 3.1 %last.1 = f32[64,4096]{1,0:T(8,128)} custom-call(s32[1,4]{1,0:T(1,128)} %bitcast.17, bf16[512,128]{1,0:T(8,128)(2,1)S(1)} %get-tuple-element.10.right_ref, bf16[4,64,512]{2,1,0:T(8,128)(2,1)S(1)} %get-tuple-element.11.weight_ref, bf16[4,128,1024]{2,1,0:T(8,128)(2,1)S(1)} %get-tuple-element.12.left_ref, f32[4,1,64,1024]{3,2,1,0:T(8,128)S(1)} %get-tuple-element.13.near_ref, ...), custom_call_target="tpu_custom_call" | custom-call | tf_op jit(solution)/shard_map/last/pallas_call | solution.py:490

commit v2 on v1

--- a/solution.py
+++ b/solution.py
@@ -19,6 +19,7 @@
 MESH = pl.DeviceIdType.MESH
 NT = (((1,), (1,)), ((), ()))
 TILE = 512
+HALF = 256
 
 
 def scale_of(features):
@@ -63,29 +64,48 @@
     return jnp.concatenate(rows, axis=1)
 
 
-def pick_rows(index_of, rows_ref, skel_ref, index_ref):
+def pick_rows(index_of, rows_ref, skel_ref, index_ref, start, count):
     width = rows_ref.shape[1]
-    for at in range(SKEL):
+    for at in range(start, start + count):
         index = index_of(at)
         skel_ref[at : at + 1, :] = rows_ref[index][None]
         index_ref[at : at + 1, :] = jnp.full((1, width), index, jnp.int32)
 
 
-def run_tiles(features, tiles):
-    held = None
-    for exponent, use in tiles:
-        value = exponent()
-        if held is not None:
-            held[1](dense_of(held[0], features).astype(BF))
-        held = (value, use)
-    held[1](dense_of(held[0], features).astype(BF))
+def partner_of(slab, step):
+    flips = [1 << at for at in range(step.bit_length()) if step >> at & 1]
+    return slab + sum((1 - 2 * (slab // flip % 2)) * flip for flip in flips)
+
+
+def tile_steps(features, tiles):
+    held = []
+
+    def step(tile):
+        value = tile[0]() if tile else None
+        if held:
+            exponent, use = held.pop()
+            use(dense_of(exponent, features))
+        if tile:
+            held.append((value, tile[1]))
+
+    return [functools.partial(step, tile) for tile in [*tiles, None]]
+
+
+def run(*streams):
+    marked = [
+        ((at + 0.5) / len(stream), which, step)
+        for which, stream in enumerate(streams)
+        for at, step in enumerate(stream)
+    ]
+    for _, _, step in sorted(marked, key=lambda one: one[:2]):
+        step()
 
 
 def chain_kernel(features, levels, slabs, points_in, weights_in, order_in, node_order_in, merge_in,
                  far_in, source_in, target_in,
                  out_ref, near_out_ref, left_ref, last_right_ref, last_weight_ref,
                  points_ref, weights_ref, rows_ref, picked_ref, right_ref, skel_ref, index_ref,
-                 dense_ref, total_ref, tree_ref, pt_ref, pt_held, wt_ref, wt_held,
+                 left_rows_ref, table_ref, dense_ref, share_ref, total_ref, tree_ref, pt_ref, pt_held, wt_ref, wt_held,
                  pair_pt, pair_wt, pair_rows, spread_ref, near_right_ref, far_right_ref,
                  asked_ref, send_ref, near_ref,
                  order_ref, node_order_ref, merge_ref, far_ref, target_ref, own_ref, source_ref,
@@ -121,17 +141,14 @@
     def sibling(level):
         return region + (1 - 2 * bit(level)) * 2**level
 
-    def ahead(step):
-        return lax.rem(slab + step, slabs)
-
-    def behind(step):
-        return lax.rem(slab + slabs - step, slabs)
+    def partner(step):
+        return partner_of(slab, step)
 
     barrier = pltpu.get_barrier_semaphore()
     for level in range(levels):
         pl.semaphore_signal(barrier, inc=1, device_id=(sibling(level), slab), device_id_type=MESH)
     for step in range(1, slabs):
-        pl.semaphore_signal(barrier, inc=1, device_id=(region, ahead(step)), device_id_type=MESH)
+        pl.semaphore_signal(barrier, inc=1, device_id=(region, partner(step)), device_id_type=MESH)
 
     def to_sibling(level, source, target, send, recv):
         return pltpu.make_async_remote_copy(
@@ -155,7 +172,7 @@
             dst_ref=asked_ref.at[step],
             send_sem=ask_send.at[step],
             recv_sem=ask_recv.at[step],
-            device_id=(region, ahead(step)),
+            device_id=(region, partner(step)),
             device_id_type=MESH,
         )
 
@@ -165,7 +182,7 @@
             dst_ref=near_ref.at[step],
             send_sem=near_send.at[step],
             recv_sem=near_recv.at[step],
-            device_id=(region, behind(step)),
+            device_id=(region, partner(step)),
             device_id_type=MESH,
         )
 
@@ -180,7 +197,7 @@
             axis=0,
         )
         rows_ref[at * SKEL : (at + 1) * SKEL, :] = both.T.astype(F32)
-    pick_rows(lambda at: order_ref[node_order_ref[at]], rows_ref, skel_ref, index_ref)
+    pick_rows(lambda at: order_ref[node_order_ref[at]], rows_ref, skel_ref, index_ref, 0, SKEL)
     skel = skel_ref[...].astype(BF).T.astype(F32)
     pt_ref[0] = skel[:features].astype(BF)
     pl.semaphore_wait(barrier, levels + slabs - 1)
@@ -188,43 +205,52 @@
     for step in range(1, slabs):
         ask_copy(step).start()
 
-    left = columns_form(skel[:features], width, True).astype(BF).T
-    table = kept_table(index_ref[...], count)
+    left_rows_ref[...] = columns_form(skel[:features], width, True).astype(BF).T
+    table_ref[...] = kept_table(index_ref[...], count)
     total_ref[...] = skel[features:]
 
-    def gather(at):
-        for inner in range(SKEL):
-            picked_ref[at * SKEL + inner : at * SKEL + inner + 1, :] = rows_ref[
-                order_ref[at * SKEL + inner]
-            ][None]
-
-    def absorb(at):
+    def zero_dense(at):
+        columns = slice(at * SKEL, (at + 1) * SKEL)
+        right = columns_form(points_ref[:, columns].astype(F32), width, False).astype(BF)
+        dense = dense_of(
+            jnp.dot(left_rows_ref[...], right, preferred_element_type=F32), features
+        )
+        dense_ref[at % 2] = dense
+        share_ref[at % 2] = kept_row(table_ref, at * SKEL, SKEL) / jnp.sum(
+            dense, axis=0, keepdims=True
+        )
+
+    def zero_spread(at):
         total_ref[...] += lax.dot_general(
             weights_ref[:, at * SKEL : (at + 1) * SKEL],
-            dense_ref[at % 2],
+            (dense_ref[at % 2] * share_ref[at % 2]).astype(BF),
             NT,
             preferred_element_type=F32,
         )
 
-    for at in range(chunks):
-        right = columns_form(points_ref[:, at * SKEL : (at + 1) * SKEL].astype(F32), width, False)
-        dense = dense_of(jnp.dot(left, right.astype(BF), preferred_element_type=F32), features)
+    def gather(at):
+        for row in range(at * SKEL, (at + 1) * SKEL):
+            picked_ref[row : row + 1, :] = rows_ref[order_ref[row]][None]
+
+    def to_tree(at):
+        one, begin = at * SKEL // leaf, at * SKEL % leaf
+        turn = picked_ref[at * SKEL : (at + 1) * SKEL, :].astype(BF).T
+        tree_ref[one, :, begin : begin + SKEL] = turn
+        left_ref[one, :, begin : begin + SKEL] = columns_form(
+            turn[:features].astype(F32), width, True
+        ).astype(BF)
+
+    for at in range(chunks + 1):
+        if at < chunks:
+            zero_dense(at)
         if at > 0:
-            absorb(at - 1)
-        share = kept_row(table, at * SKEL, SKEL) / jnp.sum(dense, axis=0, keepdims=True)
-        dense_ref[at % 2] = (dense * share).astype(BF)
-        gather(at)
-    absorb(chunks - 1)
+            zero_spread(at - 1)
+            to_tree(at - 1)
+        if at < chunks:
+            gather(at)
+
     wt_ref[0] = total_ref[...].astype(BF)
     wt_copy(0).start()
-
-    for one in range(leaves):
-        for start in range(0, leaf, SKEL):
-            turn = picked_ref[one * leaf + start : one * leaf + start + SKEL, :].astype(BF).T
-            tree_ref[one, :, start : start + SKEL] = turn
-            left_ref[one, :, start : start + SKEL] = columns_form(
-                turn[:features].astype(F32), width, True
-            ).astype(BF)
 
     def fill(slot_ref, step, table):
         own = lax.broadcasted_iota(jnp.int32, table.shape, 1) == slab
@@ -238,31 +264,70 @@
                 for other in range(leaves)
             )
 
-    for step in range(1, slabs):
+    for step in reversed(range(1, slabs)):
         ask_copy(step).wait_recv()
         fill(send_ref, step, asked_ref[step])
         near_copy(step).start()
 
     def merge_points(level):
         upper = bit(level)
-        pair_pt[upper] = pt_ref[level]
-        pair_pt[1 - upper] = pt_held[level]
-        for half in range(2):
-            points = pair_pt[half].astype(F32)
-            right_ref[half] = columns_form(points, width, False).astype(BF)
-            pair_rows[half * SKEL : (half + 1) * SKEL, :] = columns_form(points, width, True).astype(BF).T.astype(F32)
-        pick_rows(lambda at: merge_ref[level, at], pair_rows, skel_ref, index_ref)
-        pt_ref[level + 1] = (skel_ref[...] * 0.5).astype(BF).T[:features]
-        pt_copy(level + 1).start()
-        left = skel_ref[...].astype(BF)
-        index = index_ref[...]
-        table = kept_table(index, 2 * SKEL)
-        wide = jnp.concatenate([index] * (SKEL // LANES), axis=1)
-        lanes = lax.broadcasted_iota(jnp.int32, wide.shape, 1)
-        for half in range(2):
-            dense = dense_of(jnp.dot(left, right_ref[half], preferred_element_type=F32), features)
-            share = kept_row(table, half * SKEL, SKEL) / jnp.sum(dense, axis=0, keepdims=True)
-            spread_ref[half] = jnp.where(wide == lanes + half * SKEL, 1.0, dense * share).astype(BF)
+
+        def pair():
+            pair_pt[upper] = pt_ref[level]
+            pair_pt[1 - upper] = pt_held[level]
+            for half in range(2):
+                points = pair_pt[half].astype(F32)
+                right_ref[half] = columns_form(points, width, False).astype(BF)
+                pair_rows[half * SKEL : (half + 1) * SKEL, :] = (
+                    columns_form(points, width, True).astype(BF).T.astype(F32)
+                )
+
+        def pick(start):
+            pick_rows(
+                lambda at: merge_ref[level, at], pair_rows, skel_ref, index_ref, start, HALF
+            )
+
+        def leave():
+            left_rows_ref[...] = skel_ref[...].astype(BF)
+            pt_ref[level + 1] = (skel_ref[...] * 0.5).astype(BF).T[:features]
+            pt_copy(level + 1).start()
+            table_ref[...] = kept_table(index_ref[...], 2 * SKEL)
+
+        def dense(half):
+            value = dense_of(
+                jnp.dot(left_rows_ref[...], right_ref[half], preferred_element_type=F32), features
+            )
+            dense_ref[half] = value
+            share_ref[half] = kept_row(table_ref, half * SKEL, SKEL) / jnp.sum(
+                value, axis=0, keepdims=True
+            )
+
+        def spread(half):
+            index = index_ref[...]
+            for start in range(0, SKEL, LANES):
+                columns = slice(start, start + LANES)
+                lanes = lax.broadcasted_iota(jnp.int32, index.shape, 1) + (half * SKEL + start)
+                spread_ref[half, :, columns] = jnp.where(
+                    index == lanes, 1.0, dense_ref[half, :, columns] * share_ref[half, :, columns]
+                ).astype(BF)
+
+        return [
+            [pair],
+            [functools.partial(pick, 0)],
+            [functools.partial(pick, HALF)],
+            [leave, functools.partial(dense, 0)],
+            [functools.partial(spread, 0), functools.partial(dense, 1)],
+            [functools.partial(spread, 1)],
+        ]
+
+    def beside(parts, turns, tiles):
+        for at, part in enumerate(parts):
+            share = turns if at == 0 else tile_steps(
+                features,
+                tiles[len(tiles) * (at - 1) // (len(parts) - 1) : len(tiles) * at // (len(parts) - 1)],
+            )
+
+            run(part, share)
 
     def merge_weights(level):
         upper = bit(level)
@@ -276,47 +341,53 @@
         wt_copy(level + 1).start()
 
     def near_terms(step):
-        for one in range(cap):
-            target = jnp.maximum(target_ref[one, ahead(step)], 0)
-            if step == 0:
-                origin, place_at = tree_ref, (own_ref[one, slab],)
-            else:
-                origin, place_at = near_ref, (step, one)
-            for start in range(0, leaf, SKEL):
-                points = origin[(*place_at, slice(0, features), slice(start, start + SKEL))]
-                near_right_ref[start : start + SKEL, :] = columns_form(
-                    points.astype(F32), width, False
-                ).astype(BF).T
-
-            def tile(begin, start):
-                def exponent():
-                    return jnp.dot(
-                        near_right_ref[start : start + SKEL, :],
-                        left_ref[target, :, begin : begin + TILE],
-                        preferred_element_type=F32,
-                    )
-
-                def use(dense):
-                    weight = origin[
-                        (*place_at, slice(features, width), slice(start, start + SKEL))
-                    ]
-                    term = jnp.dot(weight, dense, preferred_element_type=F32)
-                    place = near_out_ref.at[step, one, :, begin : begin + TILE]
-                    place[...] = term if start == 0 else place[...] + term
-
-                return exponent, use
-
-            run_tiles(features, [
+        slots = [near_slot(step, one) for one in range(cap)]
+        return sum([slot[0] for slot in slots], []), sum([slot[1] for slot in slots], [])
+
+    def near_slot(step, one):
+        target = jnp.maximum(target_ref[one, partner(step)], 0)
+        if step == 0:
+            origin, place_at = tree_ref, (own_ref[one, slab],)
+        else:
+            origin, place_at = near_ref, (step, one)
+
+        def turn(start):
+            points = origin[(*place_at, slice(0, features), slice(start, start + SKEL))]
+            near_right_ref[one, start : start + SKEL, :] = columns_form(
+                points.astype(F32), width, False
+            ).astype(BF).T
+
+        def tile(begin, start):
+            def exponent():
+                return jnp.dot(
+                    near_right_ref[one, start : start + SKEL, :],
+                    left_ref[target, :, begin : begin + TILE],
+                    preferred_element_type=F32,
+                )
+
+            def use(dense):
+                weight = origin[(*place_at, slice(features, width), slice(start, start + SKEL))]
+                term = jnp.dot(weight, dense.astype(BF), preferred_element_type=F32)
+                place = near_out_ref.at[step, one, :, begin : begin + TILE]
+                place[...] = term if start == 0 else place[...] + term
+
+            return exponent, use
+
+        return (
+            [functools.partial(turn, start) for start in range(0, leaf, SKEL)],
+            [
                 tile(begin, start)
                 for begin in range(0, leaf, TILE)
                 for start in range(0, leaf, SKEL)
-            ])
+            ],
+        )
 
     def far_right(level):
         return columns_form(pt_held[level].astype(F32), width, False).astype(BF).T
 
     def far_terms(level):
-        far_right_ref[...] = far_right(level)
+        def turn():
+            far_right_ref[...] = far_right(level)
 
         def tile(one, begin):
             def exponent():
@@ -328,35 +399,36 @@
 
             def use(dense):
                 weight = (wt_held[level].astype(F32) * far_ref[level, 0, one].astype(F32)).astype(BF)
-                term = jnp.dot(weight, dense, preferred_element_type=F32)
+                term = jnp.dot(weight, dense.astype(BF), preferred_element_type=F32)
                 place = out_ref.at[one, :, begin : begin + TILE]
                 place[...] = term if level == 0 else place[...] + term
 
             return exponent, use
 
-        run_tiles(features, [
-            tile(one, begin) for one in range(leaves) for begin in range(0, leaf, TILE)
-        ])
-
-    def near_ready(step):
-        if step > 0:
-            near_copy(step).wait_recv()
-        near_terms(step)
-
-    steps = iter(range(slabs))
+        return (
+            [turn],
+            [tile(one, begin) for one in range(leaves) for begin in range(0, leaf, TILE)],
+        )
+
+    def alone(terms):
+        turns, tiles = terms
+        run([*turns, *tile_steps(features, tiles)])
+
     for level in range(levels - 1):
         pt_copy(level).wait_recv()
-        merge_points(level)
-        step = next(steps, None)
-        if step is not None:
-            near_ready(step)
+        if level == 0:
+            beside(merge_points(level), *near_terms(0))
+            if slabs > 1:
+                near_copy(1).wait_recv()
+                alone(near_terms(1))
+        else:
+            beside(merge_points(level), *far_terms(level - 1))
         wt_copy(level).wait_recv()
         merge_weights(level)
-    far_terms(0)
-    for step in steps:
-        near_ready(step)
-    for level in range(1, levels - 1):
-        far_terms(level)
+    alone(far_terms(levels - 2))
+    for step in reversed(range(2, slabs)):
+        near_copy(step).wait_recv()
+        alone(near_terms(step))
     pt_copy(levels - 1).wait_recv()
     last_right_ref[...] = far_right(levels - 1)
     wt_copy(levels - 1).wait_recv()
@@ -391,17 +463,17 @@
 
         def use(dense):
             place = sum_ref.at[one, :, begin : begin + TILE]
-            place[...] += jnp.dot(weight_ref[one], dense, preferred_element_type=F32)
+            place[...] += jnp.dot(weight_ref[one], dense.astype(BF), preferred_element_type=F32)
 
         return exponent, use
 
     sum_ref[...] = prior_ref[...]
     for one in range(leaves):
-        run_tiles(features, [tile(one, begin) for begin in range(0, leaf, TILE)])
+        run(tile_steps(features, [tile(one, begin) for begin in range(0, leaf, TILE)]))
         if one == 0:
             load.wait()
             for step in range(slabs):
-                owner = lax.rem(lax.axis_index("task") + step, slabs)
+                owner = partner_of(lax.axis_index("task"), step)
                 for slot in range(target_ref.shape[0]):
                     target = target_ref[slot, owner]
 
@@ -449,7 +521,10 @@
             pltpu.VMEM((2, width, SKEL), BF),
             pltpu.VMEM((SKEL, width), F32),
             pltpu.VMEM((SKEL, width), jnp.int32),
-            pltpu.VMEM((2, SKEL, SKEL), BF),
+            pltpu.VMEM((SKEL, width), BF),
+            pltpu.VMEM((LANES, LANES), F32),
+            pltpu.VMEM((2, SKEL, SKEL), F32),
+            pltpu.VMEM((2, 1, SKEL), F32),
             pltpu.VMEM((columns, SKEL), F32),
             pltpu.VMEM((leaves, width, leaf), BF),
             pltpu.VMEM((levels, features, SKEL), BF),
@@ -460,7 +535,7 @@
             pltpu.VMEM((2, columns, SKEL), BF),
             pltpu.VMEM((2 * SKEL, width), F32),
             pltpu.VMEM((2, SKEL, SKEL), BF),
-            pltpu.VMEM((leaf, width), BF),
+            pltpu.VMEM((cap, leaf, width), BF),
             pltpu.VMEM((SKEL, width), BF),
             pltpu.VMEM((slabs, cap, slabs), jnp.int32),
             pltpu.VMEM((slabs, cap, width, leaf), BF),

time: 30.4 us -> 28.2 us (0.928)
  Pallas kernels: 30.1 us -> 27.9 us
    pallas_call x1, Pallas kernels: 27.1 us -> 24.8 us  [body(): pl.pallas_call(functools.partial(chain_kernel, features, levels, slabs),...]
where the time goes in v2:
time: 28.2 us; the launch traced here: 28 us
  Pallas kernels  27.9 us (99%)
    pallas_call x1, Pallas kernels, body(): pl.pallas_call(functools.partial(chain_kernel, features, levels, slabs),...  24.8 us
    pallas_call x1, Pallas kernels, body(): pl.pallas_call(functools.partial(last_kernel, features, slabs), out_shape...  3.04 us

profile of v2, /device:TPU:0, one launch (start us, length us, event | category | flops | bytes accessed | tf_op | source)
XLA Modules:
  0.0 28.0 jit_solution(15015079685110806090)
XLA Ops:
  0.0 24.8 %chain.1 = (f32[4,64,1024]{2,1,0:T(8,128)S(1)}, f32[4,1,64,1024]{3,2,1,0:T(8,128)S(1)}, bf16[4,128,1024]{2,1,0:T(8,128)(2,1)S(1)}, bf16[512,128]{1,0:T(8,128)(2,1)S(1)}, bf16[4,64,512]{2,1,0:T(8,128)(2,1)S(1)}) custom-call(bf16[64,4096]{1,0:T(8,128)(2,1)} %bitcast.11, bf16[64,4096]{1,0:T(8,128)(2,1)} %bitcast.12, s32[4096]{0:T(1024)} %bitcast.13, ...), custom_call_target="tpu_custom_call" | custom-call | tf_op jit(solution)/shard_map/chain/pallas_call | solution.py:505
  24.8 3.0 %last.1 = f32[64,4096]{1,0:T(8,128)} custom-call(s32[1,4]{1,0:T(1,128)} %bitcast.17, bf16[512,128]{1,0:T(8,128)(2,1)S(1)} %get-tuple-element.10.right_ref, bf16[4,64,512]{2,1,0:T(8,128)(2,1)S(1)} %get-tuple-element.11.weight_ref, bf16[4,128,1024]{2,1,0:T(8,128)(2,1)S(1)} %get-tuple-element.12.left_ref, f32[4,1,64,1024]{3,2,1,0:T(8,128)S(1)} %get-tuple-element.13.near_ref, ...), custom_call_target="tpu_custom_call" | custom-call | tf_op jit(solution)/shard_map/last/pallas_call | solution.py:565
